TPU v7x, 256 devices: a whole 4x4x8 slice. The times are simulated.
256 devices in a mesh: seq: 16 (over z_lo, x), mp: 16 (over y, z_hi, core).
Axes of the slice: x: 4, y: 4, z: 8 (z_hi: 2, z_lo: 4; z = z_hi * 4 + z_lo), core: 2. Of those that a mesh axis runs over, the one named last changes fastest.
Arguments:
- inputs: bfloat16 [8192, 7168], P('seq')
- norm_gain: float32 [7168], replicated, may hold values from 0.1 to 1.9
- qkv_weight: bfloat16 [7168, 3, 3584], P('seq', None, 'mp'), may hold values from -0.0625 to 0.0625
- adapter_down: bfloat16 [7168, 128], P('seq'), may hold values from -0.0625 to 0.0625
- adapter_up: bfloat16 [3, 128, 3584], P(None, None, 'mp'), may hold values from -0.5 to 0.5
- out_weight: bfloat16 [3584, 3584], P('mp', 'seq'), may hold values from -0.5 to 0.5
- cache_keys: bfloat16 [32, 256, 3584], P('seq', None, 'mp')
- cache_values: bfloat16 [32, 256, 3584], P('seq', None, 'mp'), may hold values from -6 to 6
- cache_lengths: int32 [4], replicated, may hold values from 1 to 2048, 5120 in all
- block_perm: int32 [32], replicated, may hold values from 0 to 31, each once
Outputs:
- block_out: bfloat16 [8192, 3584], P('seq', 'mp')
Inputs may be any that keep to these rules, and one draw needn't show every extreme that they name: `cache_lengths`: each request has at least one cached position, and some request fills all of its 8 blocks. `block_perm`: each logical block appears once.
All inputs are finite; a program needn't handle non-finite values.
Results may differ from a plain program's by a relative error of at most 0.025.
Values may be sent and summed in bfloat16 or wider, within the bound.
A program may use at most 192 MiB of HBM per device.

v0:
```python
import jax
import jax.numpy as jnp
from jax import lax
from jax.sharding import PartitionSpec as P

HD = 224
REQS = 4
QLEN = 2048


lowest = -1e30


def lookup(small_table, positions_of):
    hits = positions_of[..., None] == jnp.arange(small_table.shape[0], dtype=jnp.int32)
    return jnp.sum(jnp.where(hits, small_table, 0), axis=-1)


def query_meta(token_index, lengths):
    request = token_index // QLEN
    return (request, lookup(lengths, request) + token_index % QLEN)


def key_meta(row_index, layout, permutation, lengths):
    cache_rows, block_size, tok_dev, max_blocks = layout
    rows_dev = cache_rows + tok_dev
    device = row_index // rows_dev
    local_row = row_index % rows_dev
    block_index = (
        device * (cache_rows // block_size) + jnp.minimum(local_row, cache_rows - 1) // block_size
    )
    logical = lookup(permutation, block_index)
    request = logical // max_blocks
    position = logical % max_blocks * block_size + local_row % block_size
    cached_live = position < lookup(lengths, request)
    new_req, new_pos = query_meta(device * tok_dev + local_row - cache_rows, lengths)
    in_cache = local_row < cache_rows
    key_req = jnp.where(in_cache, jnp.where(cached_live, request, -1), new_req)
    return (key_req, jnp.where(in_cache, position, new_pos))


def attend(softmax_state, queries, query_info, key_rows, value_rows, key_info, head_dim):
    query_req, query_pos = query_info
    key_req, key_pos = key_info
    visible = (key_req[None, :] == query_req[:, None]) & (key_pos[None, :] <= query_pos[:, None])
    query_count = queries.shape[0]
    key_count = key_rows.shape[0]
    head_count = queries.shape[1] // head_dim
    summed, largest, weight_sum = softmax_state
    scores = jnp.einsum(
        "qhd,khd->hqk",
        queries.reshape(query_count, head_count, head_dim),
        key_rows.reshape(key_count, head_count, head_dim),
        preferred_element_type=jnp.float32,
    ) * head_dim ** (-0.5)
    scores = jnp.where(visible[None], scores, lowest)
    new_largest = jnp.maximum(largest, jnp.max(scores, axis=-1))
    weights = jnp.where(visible[None], jnp.exp(scores - new_largest[..., None]), 0.0)
    weight_sum = jnp.sum(weights, axis=-1)
    summed = jnp.einsum(
        "hqk,khd->hqd",
        weights.astype(jnp.bfloat16),
        value_rows.reshape(key_count, head_count, head_dim),
        preferred_element_type=jnp.float32,
    )
    return (summed, new_largest, weight_sum)


def per_device(
    inputs,
    norm_gain,
    qkv_weight,
    adapter_down,
    adapter_up,
    out_weight,
    cache_keys,
    cache_values,
    cache_lengths,
    block_perm,
):
    tok_dev = inputs.shape[0]
    widened = inputs.astype(jnp.float32)
    normed = (
        widened * lax.rsqrt(jnp.mean(widened * widened, axis=-1, keepdims=True) + 1e-05) * norm_gain
    ).astype(jnp.bfloat16)
    head_width = qkv_weight.shape[2]
    weight_rows = lax.all_gather(qkv_weight, "seq", axis=0, tiled=True)
    down_rows = lax.all_gather(adapter_down, "seq", axis=0, tiled=True)
    main_part = jnp.einsum("tr,rkc->ktc", normed, weight_rows, preferred_element_type=jnp.float32)
    low_rank = jnp.dot(normed, down_rows, preferred_element_type=jnp.float32)
    main_part, low_rank = (main_part, low_rank)
    low_rank = low_rank.astype(jnp.bfloat16)
    projected = (
        main_part
        + jnp.einsum("tr,krc->ktc", low_rank, adapter_up, preferred_element_type=jnp.float32)
    ).astype(jnp.bfloat16)
    queries = projected[0]
    new_keys = projected[1]
    new_values = projected[2]
    cycle_index = lax.axis_index("seq")
    cache_rows = cache_keys.shape[0] * cache_keys.shape[1]
    layout = (cache_rows, cache_keys.shape[1], tok_dev, block_perm.shape[0] // REQS)
    key_rows = jnp.concatenate([cache_keys.reshape(cache_rows, head_width), new_keys], axis=0)
    value_rows = jnp.concatenate([cache_values.reshape(cache_rows, head_width), new_values], axis=0)
    token_ids = jnp.arange(tok_dev, dtype=jnp.int32)
    own_info = query_meta(cycle_index * tok_dev + token_ids, cache_lengths)
    head_count = head_width // HD
    softmax_state = (
        jnp.zeros((head_count, tok_dev, HD), jnp.float32),
        jnp.full((head_count, tok_dev), lowest, jnp.float32),
        jnp.zeros((head_count, tok_dev), jnp.float32),
    )
    pieces = (
        lax.all_gather(key_rows, "seq", axis=0, tiled=True),
        lax.all_gather(value_rows, "seq", axis=0, tiled=True),
    )
    row_ids = jnp.arange(pieces[0].shape[0], dtype=jnp.int32)
    key_info = key_meta(row_ids, layout, block_perm, cache_lengths)
    softmax_state = attend(softmax_state, queries, own_info, pieces[0], pieces[1], key_info, HD)
    summed, largest, weight_sum = softmax_state
    attended = (
        (summed / weight_sum[..., None])
        .transpose(1, 0, 2)
        .reshape(tok_dev, head_width)
        .astype(jnp.bfloat16)
    )
    partial_value = jnp.dot(
        attended,
        lax.all_gather(out_weight, "seq", axis=1, tiled=True),
        preferred_element_type=jnp.float32,
    )
    return lax.psum_scatter(
        partial_value.astype(jnp.bfloat16), "mp", scatter_dimension=1, tiled=True
    )


def solution(mesh):
    in_specs = (
        P("seq", None),
        P(),
        P("seq", None, "mp"),
        P("seq", None),
        P(None, None, "mp"),
        P("mp", "seq"),
        P("seq", None, "mp"),
        P("seq", None, "mp"),
        P(),
        P(),
    )
    out_specs = P("seq", "mp")
    return jax.shard_map(
        per_device, mesh=mesh, in_specs=in_specs, out_specs=out_specs, check_vma=False
    )
```

profile of v0, /device:TPU:2, one launch (start us, length us, event | category | flops | bytes accessed | tf_op | source)
XLA Modules:
  0.0 670.6 jit_solution(3314007942279095606)
XLA Ops:
  6.5 0.7 all-gather.8.cloned.1.call-update
  7.3 2.6 copy.19
  10.0 1.0 copy.24
  11.0 4.6 fusion.5
  15.6 78.8 %all-gather.8.cloned.1.call-done = bf16[7168,128]{1,0:T(8,128)(2,1)} async-done(((bf16[448,128]{1,0:T(8,128)(2,1)}), bf16[7168,128]{1,0:T(8,128)(2,1)}) %all-gather.8.cloned.1.call-update) | async-done | bytes 1835024 | tf_op jit(solution)/shard_map/all_gather | solution.py:88
  94.4 6.3 fusion.16
  100.7 155.4 %all-gather.6.cloned.1.call-done = bf16[7168,3,224]{2,1,0:T(4,128)(2,1)} async-done(((bf16[448,3,224]{2,1,0:T(4,128)(2,1)}), bf16[7168,3,224]{2,1,0:T(4,128)(2,1)}) %all-gather.6.cloned.1.call-update) | async-done | bytes 9633808 | tf_op jit(solution)/shard_map/all_gather | solution.py:87
  256.0 21.6 %copy.20 = bf16[7168,3,224]{0,2,1:T(8,128)(2,1)} copy(bf16[7168,3,224]{2,1,0:T(4,128)(2,1)} %all-gather.6.cloned.1.call-done) | data formatting | bytes 19267584 | tf_op jit(solution)/shard_map/all_gather | solution.py:87
  277.7 10.2 %fusion.10 = f32[512,672]{0,1:S(1)} fusion(bf16[7168,672]{0,1:T(8,128)(2,1)} %bitcast.29, bf16[512,7168]{1,0:T(8,128)(2,1)} %param.10, f32[7168]{0:T(1024)S(1)} %copy-done.6, f32[512]{0:T(512)S(1)} %add_rsqrt_fusion), kind=kOutput, calls=%fused_computation.14 | convolution fusion | flops 4947181568 | bytes 18380800
  287.9 0.4 fusion.24
  288.3 0.8 pad_maximum_fusion
  289.2 0.8 pad_maximum_fusion.1
  290.1 0.8 copy.23
  290.9 0.2 reduce-scatter.2.cloned.1.call-start
  291.2 0.5 select_reduce_fusion
  291.9 0.4 select_reduce_fusion.2
  292.5 91.8 %all-gather.10.cloned.1.call-done = bf16[16384,224]{0,1:T(8,128)(2,1)} async-done(((bf16[1024,224]{0,1:T(8,128)(2,1)}), bf16[16384,224]{0,1:T(8,128)(2,1)}) %all-gather.10.cloned.1.call-update) | async-done | bytes 7340048 | tf_op jit(solution)/shard_map/all_gather | solution.py:114
  384.3 18.4 %fusion = (f32[512]{0:T(512)S(1)}, f32[512,16384]{1,0:T(8,128)}) fusion(s32[16384]{0:T(1024)S(1)} %get-tuple-element.10, s32[16384]{0:T(1024)S(1)} %get-tuple-element.9, s32[512]{0:T(512)S(1)} %fusion.49, s32[512]{0:T(512)S(1)} %add_select_fusion.9, bf16[16384,224]{0,1:T(8,128)(2,1)} %all-gather.10.cloned.1.call-done, bf16[3,512,224]{1,2,0:T(8,128)(2,1)S(1)} %fusion.24), kind=kOutput, calls=%fused_computation.3 | convolution fusion | flops 3808427520 | bytes 41261056 | tf_op jit(solution)/shard_map/qhd,khd->hqk/dot_general | solution.py:50
  402.7 16.7 %fusion.1 = f32[512]{0:T(512)S(1)} fusion(f32[512,16384]{1,0:T(8,128)} %get-tuple-element.12, f32[512]{0:T(512)S(1)} %broadcast_maximum_fusion, s32[16384]{0:T(1024)S(1)} %get-tuple-element.10, s32[16384]{0:T(1024)S(1)} %get-tuple-element.9, s32[512]{0:T(512)S(1)} %fusion.49, s32[512]{0:T(512)S(1)} %add_select_fusion.9), kind=kLoop, calls=%fused_computation.6 | loop fusion | flops 67108352 | bytes 33693696 | tf_op jit(solution)/shard_map/reduce_sum | solution.py:59
  419.4 59.4 %all-gather.12.cloned.1.call-done = bf16[16384,224]{0,1:T(8,128)(2,1)} async-done(((bf16[1024,224]{0,1:T(8,128)(2,1)}), bf16[16384,224]{0,1:T(8,128)(2,1)}) %all-gather.12.cloned.1.call-update) | async-done | bytes 7340048 | tf_op jit(solution)/shard_map/all_gather | solution.py:115
  478.7 17.6 %fusion.21 = bf16[512,224]{0,1:T(8,128)(2,1)S(1)} fusion(bf16[16384,224]{0,1:T(8,128)(2,1)} %all-gather.12.cloned.1.call-done, f32[512,16384]{1,0:T(8,128)} %get-tuple-element.12, f32[512]{0:T(512)S(1)} %broadcast_maximum_fusion, s32[16384]{0:T(1024)S(1)} %get-tuple-element.10, s32[16384]{0:T(1024)S(1)} %get-tuple-element.9, s32[512]{0:T(512)S(1)} %fusion.49, ...), kind=kOutput, calls=%fused_computation.21 | convolution fusion | flops 3825434624 | bytes 41263104 | tf_op jit(solution)/shard_map/hqk,khd->hqd/dot_general | solution.py:60
  496.3 64.7 %all-gather.14.cloned.1.call-done = bf16[224,3584]{0,1:T(8,128)(2,1)} async-done(((bf16[224,224]{0,1:T(8,128)(2,1)}), bf16[224,3584]{0,1:T(8,128)(2,1)}) %all-gather.14.cloned.1.call-update) | async-done | bytes 1605648 | tf_op jit(solution)/shard_map/all_gather | solution.py:129
  561.0 4.4 convolution_convert_fusion
  565.5 98.3 %reduce-scatter.2.cloned.1.call-done = bf16[512,224]{0,1:T(8,128)(2,1)} async-done(((bf16[512,3584]{0,1:T(8,128)(2,1)}), bf16[512,224]{0,1:T(8,128)(2,1)}) %reduce-scatter.2.cloned.1.call-update) | async-done | bytes 229392 | tf_op jit(solution)/shard_map/reduce_scatter | solution.py:132
  (34 shorter events, 0.7 us)
Async XLA Ops:
  6.5 87.8 %copy-start = (bf16[3,128,224]{1,2,0:T(8,128)(2,1)S(1)}, bf16[3,128,224]{1,2,0:T(8,128)(2,1)}, u32[]{:S(2)}) copy-start(bf16[3,128,224]{1,2,0:T(8,128)(2,1)} %param.14) | copy-start | bytes 516100
  6.5 87.8 %copy-start.6 = (f32[7168]{0:T(1024)S(1)}, f32[7168]{0:T(1024)}, u32[]{:S(2)}) copy-start(f32[7168]{0:T(1024)} %param.11) | copy-start | bytes 86020
  6.5 87.8 %all-gather.8.cloned.1.call-start = ((), (), s32[]{:S(2)}) async-start(), calls=%async_computation.2 | async-start | bytes 1949696 | tf_op jit(solution)/shard_map/all_gather | solution.py:88
  7.3 248.8 %all-gather.6.cloned.1.call-start = ((), (), s32[]{:S(2)}) async-start(), calls=%async_computation.1 | async-start | bytes 15597568 | tf_op jit(solution)/shard_map/all_gather | solution.py:87
  9.9 374.4 %all-gather.10.cloned.1.call-start = ((), (), s32[]{:S(2)}) async-start(), calls=%async_computation.3 | async-start | bytes 7798784 | tf_op jit(solution)/shard_map/all_gather | solution.py:114
  277.7 11.5 %copy-start.2 = (bf16[2,256,224]{1,2,0:T(8,128)(2,1)S(1)}, bf16[2,256,224]{1,2,0:T(8,128)(2,1)}, u32[]{:S(2)}) copy-start(bf16[2,256,224]{1,2,0:T(8,128)(2,1)} %param.17) | copy-start | bytes 688132
  277.7 12.4 %copy-start.3 = (bf16[224,224]{1,0:T(8,128)(2,1)S(1)}, bf16[224,224]{1,0:T(8,128)(2,1)}, u32[]{:S(2)}) copy-start(bf16[224,224]{1,0:T(8,128)(2,1)} %param.15) | copy-start | bytes 301060
  277.7 13.5 %copy-start.5 = (s32[32]{0:T(128)S(1)}, s32[32]{0:T(128)}, u32[]{:S(2)}) copy-start(s32[32]{0:T(128)} %param.19) | copy-start | bytes 388
  277.7 14.1 %copy-start.4 = (s32[4]{0:T(128)S(1)}, s32[4]{0:T(128)}, u32[]{:S(2)}) copy-start(s32[4]{0:T(128)} %param.18) | copy-start | bytes 52
  289.1 189.6 %all-gather.12.cloned.1.call-start = ((), (), s32[]{:S(2)}) async-start(), calls=%async_computation.4 | async-start | bytes 7798784 | tf_op jit(solution)/shard_map/all_gather | solution.py:115
  290.1 270.9 %all-gather.14.cloned.1.call-start = ((), (), s32[]{:S(2)}) async-start(), calls=%async_computation.5 | async-start | bytes 1949696 | tf_op jit(solution)/shard_map/all_gather | solution.py:129
  290.9 372.9 %reduce-scatter.2.cloned.1.call-start = ((), (), s32[]{:S(2)}) async-start(), calls=%async_computation.6 | async-start | bytes 3899392 | tf_op jit(solution)/shard_map/reduce_scatter | solution.py:132
  478.7 185.0 %copy-start.1 = (bf16[3,128,224]{1,2,0:T(8,128)(2,1)S(1)}, bf16[3,128,224]{1,2,0:T(8,128)(2,1)}, u32[]{:S(2)}) copy-start(bf16[3,128,224]{1,2,0:T(8,128)(2,1)} %param.14) | copy-start | bytes 516100
Sparse Core Ops, SparseCore 0:
  9.1 85.1 all-gather.7
  96.2 159.8 all-gather.5
  289.3 95.0 all-gather.9
  386.0 92.7 all-gather.11
  480.4 80.6 all-gather.13
  565.6 98.1 reduce-scatter.1
where the time goes:
time: 672 us; the launch traced here: 671 us
  waiting for transfers between devices  549 us (82%)
  matrix products  56.8 us (8%)
  local copies, waits for them, and re-layouts  26 us (4%)
  other arithmetic  24.6 us (4%)
  between operations  13.6 us (2%)
    all_gather x1, waiting for transfers between devices, per_device(): weight_rows = lax.all_gather(qkv_weight, 'seq', axis=0, tiled=True)  155 us
    reduce_scatter x1, waiting for transfers between devices, per_device(): lax.psum_scatter(partial_value.astype(jnp.bfloat16), 'mp', scatter_dimens...  98.3 us
    all_gather x1, waiting for transfers between devices, per_device(): lax.all_gather(key_rows, 'seq', axis=0, tiled=True)  91.8 us
    all_gather x1, waiting for transfers between devices, per_device(): down_rows = lax.all_gather(adapter_down, 'seq', axis=0, tiled=True)  78.8 us
    all_gather x1, waiting for transfers between devices, per_device(): lax.all_gather(out_weight, 'seq', axis=1, tiled=True)  64.7 us
    all_gather x1, waiting for transfers between devices, per_device(): lax.all_gather(value_rows, 'seq', axis=0, tiled=True)  59.4 us
    all_gather x1, local copies, waits for them, and re-layouts, per_device(): weight_rows = lax.all_gather(qkv_weight, 'seq', axis=0, tiled=True)  21.6 us
    dot_general x1, matrix products, attend(): jnp.einsum('qhd,khd->hqk', queries.reshape(query_count, head_count, head_...  18.4 us
  transfers between devices with their start and end apart: 6, of which 6 were waited for; matrix products, arithmetic and copies ran while one was open for 10% of the time, Pallas kernels for 0%

commit v1 on v0

v1 whole, which is shorter than its diff:
```python
import functools

import jax
import jax.numpy as jnp
from jax import lax
from jax.experimental import pallas as pl
from jax.experimental.pallas import tpu as pltpu
from jax.sharding import PartitionSpec as P

HD = 224
REQS = 4
NX = 4
NZ = 4
EPS = 1e-05
LOWEST = -1e30
VMEM_LIMIT = 60 * 1024 * 1024
F32 = jnp.float32
BF16 = jnp.bfloat16


def seq_dev(z, x):
    return {"seq": z * NX + x}


def mp_dev(y, zh, core):
    return {"mp": y * 4 + zh * 2 + core}


def greet(devices, conditions):
    barrier = pltpu.get_barrier_semaphore()
    count = jnp.int32(0)
    for device, condition in zip(devices, conditions):
        if condition is None:
            pl.semaphore_signal(barrier, inc=1, device_id=device, device_id_type=pl.DeviceIdType.MESH)
            count = count + 1
        else:

            @pl.when(condition)
            def _():
                pl.semaphore_signal(barrier, inc=1, device_id=device, device_id_type=pl.DeviceIdType.MESH)

            count = count + condition.astype(jnp.int32)
    pl.semaphore_wait(barrier, count)


def remote(src, dst, send_sem, recv_sem, device):
    return pltpu.make_async_remote_copy(
        src_ref=src, dst_ref=dst, send_sem=send_sem, recv_sem=recv_sem,
        device_id=device, device_id_type=pl.DeviceIdType.MESH,
    )


def gather_kernel(
    table, x_hbm, gain_ref, w_hbm, ck_hbm, cv_hbm, ow_hbm,
    proj_ref, kv_ref, og_ref,
    xin, wall, row_kv, up, down, acc,
    load_sem, x_sem, w_recv, w_send, zw_send, o_recv, o_send, zo_send,
    c_recv, c_send, m_recv, m_send, f_recv, f_send,
):
    me = lax.axis_index("seq")
    z, x = me // NX, me % NX
    right, left, opp = (x + 1) % NX, (x + 3) % NX, (x + 2) % NX
    shard = w_hbm.shape[1]
    tok = xin.shape[0]
    half = shard // 2
    o_rows = og_ref.shape[1]
    o_half = o_rows // 2

    def wrows(s, part):
        return wall.at[:, pl.ds(pl.multiple_of(s * shard + part * half, 16), half), :]

    def orows(s, part):
        return og_ref.at[s, pl.ds(part * o_half, o_half), :]

    loads = [
        pltpu.make_async_copy(ck_hbm, row_kv.at[0, x], load_sem.at[0]),
        pltpu.make_async_copy(cv_hbm, row_kv.at[1, x], load_sem.at[1]),
        pltpu.make_async_copy(
            w_hbm, wall.at[:, pl.ds(pl.multiple_of(me * shard, 16), shard), :], load_sem.at[2]
        ),
        pltpu.make_async_copy(ow_hbm, og_ref.at[me], load_sem.at[3]),
        pltpu.make_async_copy(x_hbm, xin, x_sem),
    ]
    for load in loads:
        load.start()

    greet(
        [seq_dev(z, right), seq_dev(z, left), seq_dev(jnp.minimum(z + 1, NZ - 1), x), seq_dev(jnp.maximum(z - 1, 0), x)],
        [None, None, z < NZ - 1, z > 0],
    )

    def c_copy(kind, xs, way):
        target = right if way == 0 else left
        return remote(
            row_kv.at[kind, xs], row_kv.at[kind, xs],
            c_send.at[kind, way, 0 if xs is x else 1], c_recv.at[kind, xs], seq_dev(z, target),
        )

    loads[0].wait()
    loads[1].wait()
    for kind in (0, 1):
        for way in (0, 1):
            c_copy(kind, x, way).start()

    loads[2].wait()

    def order(j):
        zz = jnp.where(z < 2, z, 3 - z)
        o = zz if j == 0 else (1 - zz if j == 1 else j)
        return jnp.where(z < 2, o, 3 - o)

    def w_copy(s, part, send, device):
        return remote(wrows(s, part), wrows(s, part), send, w_recv.at[s, part], device)

    def o_copy(s, part, send, device):
        return remote(orows(s, part), orows(s, part), send, o_recv.at[s, part], device)

    def z_start(copy, sends, j):
        zs = order(j)
        s = zs * NX + x
        for way in (0, 1):
            zt = z + 1 if way == 0 else z - 1
            inside = (zt >= 0) & (zt < NZ)
            if j > 0:
                inside = inside & ((zs < z) if way == 0 else (zs > z))

            @pl.when(inside)
            def _():
                for part in (0, 1):
                    copy(s, part, sends.at[j, part, way], seq_dev(zt, x)).start()

    def z_finish(copy, sends):
        for j in range(NZ):
            zs = order(j)
            s = zs * NX + x
            for way in (0, 1):
                zt = z + 1 if way == 0 else z - 1
                inside = (zt >= 0) & (zt < NZ)
                if j > 0:
                    inside = inside & ((zs < z) if way == 0 else (zs > z))

                @pl.when(inside)
                def _():
                    for part in (0, 1):
                        copy(s, part, sends.at[j, part, way], seq_dev(zt, x)).wait_send()

    def z_arrive(copy, sends, j):
        s = order(j) * NX + x
        for part in (0, 1):
            copy(s, part, sends.at[j, part, 0], seq_dev(z, right)).wait_recv()

    def x_own(copy, sends, j):
        s = order(j) * NX + x
        for part in (0, 1):
            copy(s, part, sends.at[j, part, 0], seq_dev(z, right)).start()
            copy(s, part, sends.at[j, part, 1], seq_dev(z, left)).start()

    def x_near(copy, sends, j):
        row = order(j) * NX
        for part in (0, 1):
            source, target = (left, right) if part == 0 else (right, left)
            other = right if part == 0 else left
            copy(row + source, part, sends.at[j, part, 2], seq_dev(z, target)).wait_recv()
            copy(row + source, part, sends.at[j, part, 2], seq_dev(z, target)).start()
        for part in (0, 1):
            other = right if part == 0 else left
            copy(row + other, part, sends.at[j, part, 2], seq_dev(z, right)).wait_recv()

    def x_far(copy, sends, j):
        row = order(j) * NX
        for part in (0, 1):
            copy(row + opp, part, sends.at[j, part, 2], seq_dev(z, right)).wait_recv()

    def x_finish(copy, sends):
        for j in range(NZ):
            row = order(j) * NX
            for part in (0, 1):
                copy(row + x, part, sends.at[j, part, 0], seq_dev(z, right)).wait_send()
                copy(row + x, part, sends.at[j, part, 1], seq_dev(z, left)).wait_send()
                source = left if part == 0 else right
                copy(row + source, part, sends.at[j, part, 2], seq_dev(z, right)).wait_send()

    z_start(w_copy, zw_send, 0)

    loads[4].wait()

    @pl.loop(0, tok // 16)
    def _(i):
        rows = pl.ds(pl.multiple_of(i * 16, 16), 16)
        wide = xin[rows, :].astype(F32)
        mean = jnp.mean(wide * wide, axis=-1, keepdims=True)
        xin[rows, :] = (wide * lax.rsqrt(mean + EPS) * gain_ref[...]).astype(BF16)

    for kind in (0, 1):
        source = left if kind == 0 else right
        c_copy(kind, source, kind).wait_recv()
        c_copy(kind, source, kind).start()
    x_own(w_copy, w_send, 0)
    for kind in (0, 1):
        c_copy(kind, right if kind == 0 else left, 0).wait_recv()
    for kind in (0, 1):
        c_copy(kind, opp, 0).wait_recv()

    def held(kind, d, i):
        return row_kv[kind, table[8 + 2 * d + i] // 2, table[8 + 2 * d + i] % 2]

    def message(buffer, way, d, kind):
        return remote(
            buffer.at[d, kind], buffer.at[d, kind], m_send.at[way, d, kind], m_recv.at[way, d, kind],
            seq_dev(jnp.clip(z + 1 - 2 * way, 0, NZ - 1), x),
        )

    def relay(way, hop):
        buffer = up if way == 0 else down
        here = hop if way == 0 else NZ - 1 - hop

        @pl.when(z == here)
        def _():
            passing = range(NZ - 1, here, -1) if way == 0 else range(0, here)
            for d in passing:
                for kind in (0, 1):
                    if hop > 0:
                        message(buffer, way, d, kind).wait_recv()
                    for i in (0, 1):
                        if hop == 0:
                            buffer[d, kind, i] = held(kind, d, i)
                        else:
                            buffer[d, kind, i] = jnp.where(
                                table[2 * d + i] == here, held(kind, d, i), buffer[d, kind, i]
                            )
                    message(buffer, way, d, kind).start()
            if hop > 0:
                for kind in (0, 1):
                    message(buffer, way, here, kind).wait_recv()

    def relay_finish(way):
        buffer = up if way == 0 else down
        for here in range(NZ):
            passing = range(NZ - 1, here, -1) if way == 0 else range(0, here)

            @pl.when(z == here)
            def _():
                for d in passing:
                    for kind in (0, 1):
                        message(buffer, way, d, kind).wait_send()

    def multiply(j):
        zs = order(j)
        width = NX * shard
        span = pl.ds(pl.multiple_of(zs * width, 128), width)

        @pl.loop(0, tok // 128)
        def _(i):
            rows = pl.ds(pl.multiple_of(i * 128, 128), 128)
            for k in range(3):
                got = jnp.dot(
                    xin[rows, span], wall[k, pl.ds(pl.multiple_of(zs * width, 16), width), :],
                    preferred_element_type=F32,
                )
                if j == 0:
                    acc[k, rows, :] = got
                elif j < NZ - 1:
                    acc[k, rows, :] += got
                else:
                    proj_ref[k, rows, :] = (acc[k, rows, :] + got).astype(BF16)

    relay(0, 0)
    relay(1, 0)
    z_arrive(w_copy, zw_send, 1)
    z_start(w_copy, zw_send, 1)
    x_own(w_copy, w_send, 1)
    x_near(w_copy, w_send, 0)
    relay(0, 1)
    relay(1, 1)
    z_arrive(w_copy, zw_send, 2)
    z_start(w_copy, zw_send, 2)
    x_own(w_copy, w_send, 2)
    loads[3].wait()
    z_start(o_copy, zo_send, 0)
    x_far(w_copy, w_send, 0)
    multiply(0)
    x_near(w_copy, w_send, 1)
    relay(0, 2)
    relay(1, 2)
    z_arrive(w_copy, zw_send, 3)
    z_start(w_copy, zw_send, 3)
    x_own(w_copy, w_send, 3)
    x_far(w_copy, w_send, 1)
    multiply(1)
    x_near(w_copy, w_send, 2)
    relay(0, 3)
    relay(1, 3)

    for kind in (0, 1):
        for i in (0, 1):
            low = up[z, kind, i]
            high = down[z, kind, i]
            origin = table[2 * z + i]
            kv_ref[kind, 2 * x + i] = jnp.where(
                origin == z, held(kind, z, i), jnp.where(origin < z, low, high)
            )

    def f_copy(kind, xs, slot, target):
        ref = kv_ref.at[kind, pl.ds(2 * xs, 2)]
        return remote(ref, ref, f_send.at[kind, slot], f_recv.at[kind, xs], seq_dev(z, target))

    for kind in (0, 1):
        f_copy(kind, x, 0, right).start()
        f_copy(kind, x, 1, left).start()
    x_own(o_copy, o_send, 0)
    for j in (1, 2, 3):
        z_arrive(o_copy, zo_send, j)
        z_start(o_copy, zo_send, j)
        x_own(o_copy, o_send, j)
    x_far(w_copy, w_send, 2)
    multiply(2)
    x_near(w_copy, w_send, 3)
    for kind in (0, 1):
        source, target = (left, right) if kind == 0 else (right, left)
        f_copy(kind, source, 2, target).wait_recv()
        f_copy(kind, source, 2, target).start()
    for j in range(NZ):
        x_near(o_copy, o_send, j)
    x_far(w_copy, w_send, 3)
    multiply(3)
    for kind in (0, 1):
        f_copy(kind, right if kind == 0 else left, 2, right).wait_recv()
        f_copy(kind, opp, 2, right).wait_recv()
    for j in range(NZ):
        x_far(o_copy, o_send, j)

    for kind in (0, 1):
        for way in (0, 1):
            c_copy(kind, x, way).wait_send()
        c_copy(kind, left if kind == 0 else right, kind).wait_send()
        for slot in range(3):
            f_copy(kind, x, slot, right).wait_send()
    relay_finish(0)
    relay_finish(1)
    z_finish(w_copy, zw_send)
    x_finish(w_copy, w_send)
    z_finish(o_copy, zo_send)
    x_finish(o_copy, o_send)


def attend_kernel(
    length, proj_ref, kv_ref, og_ref, out_ref,
    near, top, total, mixed, attended, parts, mates, ring, sums,
    k_recv, k_send, a_recv, a_send, y_recv, y_send, h_recv, h_send,
):
    me = lax.axis_index("seq")
    mp = lax.axis_index("mp")
    z, x = me // NX, me % NX
    right, left, opp = (x + 1) % NX, (x + 3) % NX, (x + 2) % NX
    y, zh, core = mp // 4, (mp // 2) % 2, mp % 2
    y_up, y_dn, y_opp = (y + 1) % 4, (y + 3) % 4, (y + 2) % 4
    tok = proj_ref.shape[1]

    greet(
        [seq_dev(z, right), seq_dev(z, left), mp_dev(y, zh, 1 - core), mp_dev(y_up, zh, core), mp_dev(y_dn, zh, core), mp_dev(y, 1 - zh, core)],
        [None] * 6,
    )

    def k_copy(kind, xs, slot, target):
        src = proj_ref.at[1 + kind] if xs is x else near.at[kind, xs]
        return remote(src, near.at[kind, xs], k_send.at[kind, slot], k_recv.at[kind, xs], seq_dev(z, target))

    for kind in (0, 1):
        k_copy(kind, x, 0, right).start()
        k_copy(kind, x, 1, left).start()

    scale = HD ** (-0.5)

    def update(keys, values, mask, first=False):
        scores = lax.dot_general(
            proj_ref[0], keys, (((1,), (1,)), ((), ())), preferred_element_type=F32
        ) * scale
        if mask is not None:
            scores = jnp.where(mask, scores, LOWEST)
        largest = jnp.max(scores, axis=-1, keepdims=True)
        if not first:
            largest = jnp.maximum(largest, top[...])
        weights = jnp.exp(scores - largest)
        weight_sum = jnp.sum(weights, axis=-1, keepdims=True)
        got = jnp.dot(weights.astype(BF16), values, preferred_element_type=F32)
        if first:
            total[...] = weight_sum
            mixed[...] = got
        else:
            fade = jnp.exp(top[...] - largest)
            total[...] = total[...] * fade + weight_sum
            mixed[...] = mixed[...] * fade + got
        top[...] = largest

    columns = lax.broadcasted_iota(jnp.int32, (tok, 512), 1)
    update(
        kv_ref[0, 0:2].reshape(512, HD), kv_ref[1, 0:2].reshape(512, HD), columns < length[0], True
    )

    @pl.loop(1, 4)
    def _(c):
        two = pl.ds(2 * c, 2)
        ids = lax.broadcasted_iota(jnp.int32, (tok, 512), 1) + c * 512
        update(kv_ref[0, two].reshape(512, HD), kv_ref[1, two].reshape(512, HD), ids < length[0])

    rows = lax.broadcasted_iota(jnp.int32, (tok, tok), 0)
    update(proj_ref[1], proj_ref[2], columns <= rows)

    for kind in (0, 1):
        source, target = (left, right) if kind == 0 else (right, left)
        k_copy(kind, source, 2, target).wait_recv()
        k_copy(kind, source, 2, target).start()
    for kind in (0, 1):
        k_copy(kind, right if kind == 0 else left, 2, right).wait_recv()

    @pl.when(x > 0)
    def _():
        update(near[0, left], near[1, left], None)

    @pl.when(x == NX - 1)
    def _():
        update(near[0, right], near[1, right], None)

    for kind in (0, 1):
        k_copy(kind, opp, 2, right).wait_recv()

    @pl.when(x > 1)
    def _():
        update(near[0, opp], near[1, opp], None)

    attended[...] = (mixed[...] / total[...]).astype(BF16)

    @pl.loop(0, 8)
    def _(c):
        parts[c] = jnp.dot(
            attended[...], og_ref[2 * c + 1 - core], preferred_element_type=F32
        ).astype(BF16)

    mate = remote(parts, mates, a_send, a_recv, mp_dev(y, zh, 1 - core))
    mate.start()

    @pl.loop(0, 8)
    def _(c):
        sums[c] = jnp.dot(attended[...], og_ref[2 * c + core], preferred_element_type=F32).astype(BF16)

    mate.wait_recv()

    @pl.loop(0, 8)
    def _(c):
        sums[c] = (sums[c].astype(F32) + mates[c].astype(F32)).astype(BF16)

    def far(way):
        target = y_up if way == 0 else y_dn
        return remote(
            sums.at[2 * y_opp + way], ring.at[way, 0], y_send.at[way, 0], y_recv.at[way, 0],
            mp_dev(target, zh, core),
        )

    def close(way, h):
        target = y_up if way == 0 else y_dn
        return remote(
            sums.at[2 * target + h], ring.at[way, 1 + h], y_send.at[way, 1 + h], y_recv.at[way, 1 + h],
            mp_dev(target, zh, core),
        )

    far(0).start()
    far(1).start()
    for way in (0, 1):
        close(way, 1 - way).start()
    for way in (0, 1):
        target = y_up if way == 0 else y_dn
        far(way).wait_recv()
        sums[2 * target + way] = (
            sums[2 * target + way].astype(F32) + ring[way, 0].astype(F32)
        ).astype(BF16)
        close(way, way).start()
    for way in (0, 1):
        for h in (0, 1):
            close(way, h).wait_recv()

    def chunk(h):
        return sums[2 * y + h].astype(F32) + ring[0, 1 + h].astype(F32) + ring[1, 1 + h].astype(F32)

    attended[...] = jnp.where(zh == 0, chunk(1), chunk(0)).astype(BF16)
    last = remote(attended, near.at[0, x], h_send, h_recv, mp_dev(y, 1 - zh, core))
    last.start()
    mine = jnp.where(zh == 0, chunk(0), chunk(1))
    last.wait_recv()
    out_ref[...] = (mine + near[0, x].astype(F32)).astype(BF16)

    for kind in (0, 1):
        for slot in range(3):
            k_copy(kind, x, slot, right).wait_send()
    mate.wait_send()
    for way in (0, 1):
        far(way).wait_send()
        close(way, 0).wait_send()
        close(way, 1).wait_send()
    last.wait_send()


def vmem():
    return pl.BlockSpec(memory_space=pltpu.VMEM)


def smem():
    return pl.BlockSpec(memory_space=pltpu.SMEM)


def hbm():
    return pl.BlockSpec(memory_space=pl.ANY)


def per_device(
    inputs, norm_gain, qkv_weight, adapter_down, adapter_up, out_weight,
    cache_keys, cache_values, cache_lengths, block_perm,
):
    tok, d_in = inputs.shape
    shard = qkv_weight.shape[0]
    blk = cache_keys.shape[1]
    dma = pltpu.SemaphoreType.DMA
    me = lax.axis_index("seq")
    z, x = me // NX, me % NX

    folded = (
        qkv_weight.transpose(1, 0, 2).astype(F32)
        + jnp.einsum("rj,kjc->krc", adapter_down, adapter_up, preferred_element_type=F32)
    ).astype(BF16)

    logical = jnp.arange(NZ, dtype=jnp.int32)[:, None] * 8 + 2 * x + jnp.arange(2, dtype=jnp.int32)[None, :]
    count = block_perm.shape[0]
    hits = block_perm[None, :] == logical.reshape(-1)[:, None]
    place = jnp.sum(jnp.where(hits, jnp.arange(count, dtype=jnp.int32)[None, :], 0), axis=-1)
    table = jnp.concatenate([place // 8, place % 8]).astype(jnp.int32)
    length = jnp.sum(
        jnp.where(jnp.arange(REQS, dtype=jnp.int32) == z, cache_lengths, 0)
    ).reshape(1)

    proj, kv, og = pl.pallas_call(
        gather_kernel,
        out_shape=(
            jax.ShapeDtypeStruct((3, tok, HD), BF16),
            jax.ShapeDtypeStruct((2, 8, blk, HD), BF16),
            jax.ShapeDtypeStruct((16, HD, HD), BF16),
        ),
        in_specs=[smem(), hbm(), vmem(), hbm(), hbm(), hbm(), hbm()],
        out_specs=(vmem(), vmem(), vmem()),
        scratch_shapes=[
            pltpu.VMEM((tok, d_in), BF16),
            pltpu.VMEM((3, d_in, HD), BF16),
            pltpu.VMEM((2, NX, 2, blk, HD), BF16),
            pltpu.VMEM((NZ, 2, 2, blk, HD), BF16),
            pltpu.VMEM((NZ, 2, 2, blk, HD), BF16),
            pltpu.VMEM((3, tok, HD), F32),
            dma((4,)), dma,
            dma((16, 2)), dma((4, 2, 3)), dma((4, 2, 2)),
            dma((16, 2)), dma((4, 2, 3)), dma((4, 2, 2)),
            dma((2, 4)), dma((2, 2, 2)),
            dma((2, 4, 2)), dma((2, 4, 2)),
            dma((2, 4)), dma((2, 3)),
        ],
        compiler_params=pltpu.CompilerParams(
            collective_id=0, has_side_effects=True, vmem_limit_bytes=VMEM_LIMIT
        ),
        name="gather",
    )(table, inputs, norm_gain.reshape(1, d_in), folded, cache_keys, cache_values, out_weight)

    return pl.pallas_call(
        attend_kernel,
        out_shape=jax.ShapeDtypeStruct((tok, HD), BF16),
        in_specs=[smem(), vmem(), vmem(), vmem()],
        out_specs=vmem(),
        scratch_shapes=[
            pltpu.VMEM((2, NX, tok, HD), BF16),
            pltpu.VMEM((tok, 1), F32),
            pltpu.VMEM((tok, 1), F32),
            pltpu.VMEM((tok, HD), F32),
            pltpu.VMEM((tok, HD), BF16),
            pltpu.VMEM((8, tok, HD), BF16),
            pltpu.VMEM((8, tok, HD), BF16),
            pltpu.VMEM((2, 3, tok, HD), BF16),
            pltpu.VMEM((8, tok, HD), BF16),
            dma((2, 4)), dma((2, 3)),
            dma, dma,
            dma((2, 3)), dma((2, 3)),
            dma, dma,
        ],
        compiler_params=pltpu.CompilerParams(
            collective_id=1, has_side_effects=True, vmem_limit_bytes=VMEM_LIMIT
        ),
        name="attend",
    )(length, proj, kv, og)


def solution(mesh):
    in_specs = (
        P("seq", None), P(), P("seq", None, "mp"), P("seq", None), P(None, None, "mp"),
        P("mp", "seq"), P("seq", None, "mp"), P("seq", None, "mp"), P(), P(),
    )
    return jax.shard_map(
        per_device, mesh=mesh, in_specs=in_specs, out_specs=P("seq", "mp"), check_vma=False
    )
```

time: 672 us -> 241 us (0.36)
  waiting for transfers between devices: 549 us -> 0 us
  Pallas kernels: 0 us -> 227 us
  matrix products: 56.8 us -> 2.39 us
  other arithmetic: 24.6 us -> 2.85 us
  local copies, waits for them, and re-layouts: 26 us -> 5.44 us
  between operations: 13.6 us -> 0.02 us
    all_gather x5 -> x0, waiting for transfers between devices: 450 us -> none  [the longest x1 155 us: per_device(): weight_rows = lax.all_gather(qkv_weight, 'seq', axis=0, tiled=True)]
    pallas_call x0 -> x2, Pallas kernels: none -> 227 us  [the longest x1 164 us: per_device(): pl.pallas_call(gather_kernel, out_shape=(jax.ShapeDtypeStruct((3, tok, HD...]
    reduce_scatter x1 -> x0, waiting for transfers between devices: 98.3 us -> none  [per_device(): lax.psum_scatter(partial_value.astype(jnp.bfloat16), 'mp', scatter_dimens...]
    dot_general x3 -> x1, matrix products: 40.3 us -> 2.39 us  [per_device(): jnp.einsum('rj,kjc->krc', adapter_down, adapter_up, preferred_element_typ...]
    all_gather x1 -> x0, local copies, waits for them, and re-layouts: 21.6 us -> none  [per_device(): weight_rows = lax.all_gather(qkv_weight, 'seq', axis=0, tiled=True)]
    reduce_sum x5 -> x2, other arithmetic: 22.2 us -> 2.17 us  [the longest x1 1.33 us: per_device(): jnp.sum(jnp.where(jnp.arange(REQS, dtype=jnp.int32) == z, cache_lengths, 0))]
    unnamed x2 -> x0, matrix products: 16.4 us -> none
  transfers between devices with their start and end apart: 6 -> 0, of which waited for: 6 -> 0; matrix products, arithmetic and copies ran while one was open for 10% -> 0% of each run, Pallas kernels for 0% -> 0%
where the time goes in v1:
time: 241 us; the launch traced here: 237 us
  Pallas kernels  227 us (94%)
  local copies, waits for them, and re-layouts  5.44 us (2%)
  other arithmetic  2.85 us (1%)
    pallas_call x1, Pallas kernels, per_device(): pl.pallas_call(gather_kernel, out_shape=(jax.ShapeDtypeStruct((3, tok, HD...  164 us
    pallas_call x1, Pallas kernels, per_device(): pl.pallas_call(attend_kernel, out_shape=jax.ShapeDtypeStruct((tok, HD), B...  62.7 us

profile of v1, /device:TPU:2, one launch (start us, length us, event | category | flops | bytes accessed | tf_op | source)
XLA Modules:
  0.0 237.4 jit_solution(14481895601999333561)
XLA Ops:
  0.0 0.0 copy-start
  0.0 1.3 fusion.3
  1.3 0.1 iota_add_fusion
  1.4 0.1 add.52
  1.5 0.8 select_reduce_fusion
  2.4 0.6 pad_add_fusion.table
  2.9 1.8 copy.20.ck_hbm
  4.7 1.8 copy.21.cv_hbm
  6.5 0.0 copy-done
  6.5 2.4 %fusion.1.w_hbm = bf16[3,448,224]{2,1,0:T(8,128)(2,1)} fusion(bf16[3,128,224]{1,2,0:T(8,128)(2,1)S(1)} %copy-done, bf16[448,3,224]{2,0,1:T(8,128)(2,1)} %param.12, bf16[448,128]{1,0:T(8,128)(2,1)} %param.13), kind=kOutput, calls=%fused_computation.2 | convolution fusion | flops 77973504 | bytes 1490944 | tf_op jit(solution)/shard_map/rj,kjc->krc/dot_general | solution.py:527
  8.9 164.0 %gather.1 = (bf16[3,512,224]{2,1,0:T(8,128)(2,1)}, bf16[2,8,256,224]{3,2,1,0:T(8,128)(2,1)}, bf16[16,224,224]{2,1,0:T(8,128)(2,1)}) custom-call(s32[16]{0:T(128)} %pad_add_fusion.table, bf16[512,7168]{1,0:T(8,128)(2,1)} %x_hbm.1, f32[1,7168]{1,0:T(1,128)} %bitcast.16, bf16[3,448,224]{2,1,0:T(8,128)(2,1)} %fusion.1.w_hbm, bf16[2,256,224]{2,1,0:T(8,128)(2,1)} %copy.20.ck_hbm, ...), custom_call_target="tpu_custom_call" | custom-call | tf_op jit(solution)/shard_map/gather/pallas_call | solution.py:539
  172.9 62.7 %attend.1 = bf16[512,224]{1,0:T(8,128)(2,1)} custom-call(s32[1]{0:T(128)} %bitcast.length, bf16[3,512,224]{2,1,0:T(8,128)(2,1)} %get-tuple-element.8.proj_ref, bf16[2,8,256,224]{3,2,1,0:T(8,128)(2,1)} %get-tuple-element.9.kv_ref, bf16[16,224,224]{2,1,0:T(8,128)(2,1)} %get-tuple-element.10.og_ref), custom_call_target="tpu_custom_call" | custom-call | tf_op jit(solution)/shard_map/attend/pallas_call | solution.py:568
  235.6 1.8 copy.22
  (2 shorter events, 0.0 us)
Async XLA Ops:
  0.0 6.5 %copy-start = (bf16[3,128,224]{1,2,0:T(8,128)(2,1)S(1)}, bf16[3,128,224]{1,2,0:T(8,128)(2,1)}, u32[]{:S(2)}) copy-start(bf16[3,128,224]{1,2,0:T(8,128)(2,1)} %param.14) | copy-start | bytes 516100

commit v2 on v1

--- a/solution.py
+++ b/solution.py
@@ -53,71 +53,71 @@
 def gather_kernel(
     table, x_hbm, gain_ref, w_hbm, ck_hbm, cv_hbm, ow_hbm,
     proj_ref, kv_ref, og_ref,
-    xin, wall, row_kv, up, down, acc,
-    load_sem, x_sem, w_recv, w_send, zw_send, o_recv, o_send, zo_send,
-    c_recv, c_send, m_recv, m_send, f_recv, f_send,
+    xin, xsub, nsub, turn, grid, wall, row_kv, up, down, own, pout, p_far, p_close,
+    load_sem, w_recv, zw_send, o_recv, o_send, zo_send,
+    i_recv, i_send, j_recv, j_send, y_recv, y_send, e_recv, e_send,
+    c_recv, c_send, m_recv, m_send, f_recv, f_send, r_recv, r_send, s_recv, s_send,
 ):
     me = lax.axis_index("seq")
+    mp = lax.axis_index("mp")
     z, x = me // NX, me % NX
+    y, zh, core = mp // 4, (mp // 2) % 2, mp % 2
     right, left, opp = (x + 1) % NX, (x + 3) % NX, (x + 2) % NX
+    y_up, y_dn, y_opp = (y + 1) % 4, (y + 3) % 4, (y + 2) % 4
     shard = w_hbm.shape[1]
     tok = xin.shape[0]
-    half = shard // 2
-    o_rows = og_ref.shape[1]
-    o_half = o_rows // 2
-
-    def wrows(s, part):
-        return wall.at[:, pl.ds(pl.multiple_of(s * shard + part * half, 16), half), :]
+    sub = tok // 8
+    o_half = og_ref.shape[1] // 2
+    peers = (right, left, opp)
+
+    def sub_rows(yc, cc, h=None):
+        start = (yc * 2 + cc) * sub
+        if h is None:
+            return pl.ds(pl.multiple_of(start, sub), sub)
+        return pl.ds(pl.multiple_of(start + h * (sub // 2), sub // 2), sub // 2)
+
+    def wrows(zs, k):
+        return wall.at[k, pl.ds(pl.multiple_of(zs * shard, 16), shard), :]
 
     def orows(s, part):
         return og_ref.at[s, pl.ds(part * o_half, o_half), :]
 
     loads = [
-        pltpu.make_async_copy(ck_hbm, row_kv.at[0, x], load_sem.at[0]),
-        pltpu.make_async_copy(cv_hbm, row_kv.at[1, x], load_sem.at[1]),
-        pltpu.make_async_copy(
-            w_hbm, wall.at[:, pl.ds(pl.multiple_of(me * shard, 16), shard), :], load_sem.at[2]
-        ),
-        pltpu.make_async_copy(ow_hbm, og_ref.at[me], load_sem.at[3]),
-        pltpu.make_async_copy(x_hbm, xin, x_sem),
+        pltpu.make_async_copy(w_hbm, wall.at[:, pl.ds(pl.multiple_of(z * shard, 16), shard), :], load_sem.at[0]),
+        pltpu.make_async_copy(x_hbm.at[sub_rows(y, core), :], xsub, load_sem.at[1]),
+        pltpu.make_async_copy(ck_hbm, row_kv.at[0, x], load_sem.at[2]),
+        pltpu.make_async_copy(x_hbm, xin, load_sem.at[3]),
+        pltpu.make_async_copy(cv_hbm, row_kv.at[1, x], load_sem.at[4]),
+        pltpu.make_async_copy(ow_hbm, og_ref.at[me], load_sem.at[5]),
     ]
     for load in loads:
         load.start()
 
     greet(
-        [seq_dev(z, right), seq_dev(z, left), seq_dev(jnp.minimum(z + 1, NZ - 1), x), seq_dev(jnp.maximum(z - 1, 0), x)],
-        [None, None, z < NZ - 1, z > 0],
+        [
+            seq_dev(z, right), seq_dev(z, left), seq_dev(jnp.minimum(z + 1, NZ - 1), x), seq_dev(jnp.maximum(z - 1, 0), x),
+            mp_dev(y_up, zh, core), mp_dev(y_dn, zh, core), mp_dev(y, zh, 1 - core),
+        ],
+        [None, None, z < NZ - 1, z > 0, None, None, None],
     )
-
-    def c_copy(kind, xs, way):
-        target = right if way == 0 else left
-        return remote(
-            row_kv.at[kind, xs], row_kv.at[kind, xs],
-            c_send.at[kind, way, 0 if xs is x else 1], c_recv.at[kind, xs], seq_dev(z, target),
-        )
-
-    loads[0].wait()
-    loads[1].wait()
-    for kind in (0, 1):
-        for way in (0, 1):
-            c_copy(kind, x, way).start()
-
-    loads[2].wait()
 
     def order(j):
         zz = jnp.where(z < 2, z, 3 - z)
         o = zz if j == 0 else (1 - zz if j == 1 else j)
         return jnp.where(z < 2, o, 3 - o)
 
-    def w_copy(s, part, send, device):
-        return remote(wrows(s, part), wrows(s, part), send, w_recv.at[s, part], device)
+    def w_copy(j, k, send, device):
+        zs = order(j)
+        return remote(wrows(zs, k), wrows(zs, k), send, w_recv.at[zs, k], device)
 
     def o_copy(s, part, send, device):
         return remote(orows(s, part), orows(s, part), send, o_recv.at[s, part], device)
 
-    def z_start(copy, sends, j):
+    def oz_copy(j, part, send, device):
+        return o_copy(order(j) * NX + x, part, send, device)
+
+    def z_each(j, act):
         zs = order(j)
-        s = zs * NX + x
         for way in (0, 1):
             zt = z + 1 if way == 0 else z - 1
             inside = (zt >= 0) & (zt < NZ)
@@ -126,76 +126,159 @@
 
             @pl.when(inside)
             def _():
-                for part in (0, 1):
-                    copy(s, part, sends.at[j, part, way], seq_dev(zt, x)).start()
-
-    def z_finish(copy, sends):
+                act(way, seq_dev(zt, x))
+
+    def z_start(copy, sends, j, parts):
+        z_each(j, lambda way, device: [copy(j, p, sends.at[j, p, way], device).start() for p in parts])
+
+    def z_finish(copy, sends, parts):
         for j in range(NZ):
-            zs = order(j)
-            s = zs * NX + x
-            for way in (0, 1):
-                zt = z + 1 if way == 0 else z - 1
-                inside = (zt >= 0) & (zt < NZ)
-                if j > 0:
-                    inside = inside & ((zs < z) if way == 0 else (zs > z))
-
-                @pl.when(inside)
-                def _():
-                    for part in (0, 1):
-                        copy(s, part, sends.at[j, part, way], seq_dev(zt, x)).wait_send()
-
-    def z_arrive(copy, sends, j):
+            z_each(j, lambda way, device: [copy(j, p, sends.at[j, p, way], device).wait_send() for p in parts])
+
+    def z_arrive(copy, sends, j, parts):
+        for p in parts:
+            copy(j, p, sends.at[j, p, 0], seq_dev(z, right)).wait_recv()
+
+    def w_step(j, k):
+        z_arrive(w_copy, zw_send, j, (k,))
+        z_start(w_copy, zw_send, j, (k,))
+
+    def x_own(j):
         s = order(j) * NX + x
         for part in (0, 1):
-            copy(s, part, sends.at[j, part, 0], seq_dev(z, right)).wait_recv()
-
-    def x_own(copy, sends, j):
-        s = order(j) * NX + x
-        for part in (0, 1):
-            copy(s, part, sends.at[j, part, 0], seq_dev(z, right)).start()
-            copy(s, part, sends.at[j, part, 1], seq_dev(z, left)).start()
-
-    def x_near(copy, sends, j):
+            o_copy(s, part, o_send.at[j, part, 0], seq_dev(z, right)).start()
+            o_copy(s, part, o_send.at[j, part, 1], seq_dev(z, left)).start()
+
+    def x_near(j):
         row = order(j) * NX
         for part in (0, 1):
             source, target = (left, right) if part == 0 else (right, left)
-            other = right if part == 0 else left
-            copy(row + source, part, sends.at[j, part, 2], seq_dev(z, target)).wait_recv()
-            copy(row + source, part, sends.at[j, part, 2], seq_dev(z, target)).start()
+            o_copy(row + source, part, o_send.at[j, part, 2], seq_dev(z, target)).wait_recv()
+            o_copy(row + source, part, o_send.at[j, part, 2], seq_dev(z, target)).start()
         for part in (0, 1):
-            other = right if part == 0 else left
-            copy(row + other, part, sends.at[j, part, 2], seq_dev(z, right)).wait_recv()
-
-    def x_far(copy, sends, j):
-        row = order(j) * NX
+            o_copy(row + (right if part == 0 else left), part, o_send.at[j, part, 2], seq_dev(z, right)).wait_recv()
+
+    def x_far(j):
         for part in (0, 1):
-            copy(row + opp, part, sends.at[j, part, 2], seq_dev(z, right)).wait_recv()
-
-    def x_finish(copy, sends):
+            o_copy(order(j) * NX + opp, part, o_send.at[j, part, 2], seq_dev(z, right)).wait_recv()
+
+    def x_finish():
         for j in range(NZ):
             row = order(j) * NX
             for part in (0, 1):
-                copy(row + x, part, sends.at[j, part, 0], seq_dev(z, right)).wait_send()
-                copy(row + x, part, sends.at[j, part, 1], seq_dev(z, left)).wait_send()
+                o_copy(row + x, part, o_send.at[j, part, 0], seq_dev(z, right)).wait_send()
+                o_copy(row + x, part, o_send.at[j, part, 1], seq_dev(z, left)).wait_send()
                 source = left if part == 0 else right
-                copy(row + source, part, sends.at[j, part, 2], seq_dev(z, right)).wait_send()
-
-    z_start(w_copy, zw_send, 0)
-
-    loads[4].wait()
-
-    @pl.loop(0, tok // 16)
+                o_copy(row + source, part, o_send.at[j, part, 2], seq_dev(z, right)).wait_send()
+
+    def c_copy(kind, xs, way):
+        return remote(
+            row_kv.at[kind, xs], row_kv.at[kind, xs],
+            c_send.at[kind, way, 0 if xs is x else 1], c_recv.at[kind, xs],
+            seq_dev(z, right if way == 0 else left),
+        )
+
+    half = sub // 2
+
+    def far_in(way):
+        target = right if way == 0 else left
+        return remote(
+            nsub.at[opp, pl.ds(way * half, half)], turn.at[way], i_send.at[way], i_recv.at[way], seq_dev(z, target)
+        )
+
+    def pass_in(way):
+        source, target = (left, right) if way == 0 else (right, left)
+        return remote(
+            turn.at[way], grid.at[source, sub_rows(y, core, way)], j_send.at[way], j_recv.at[way], seq_dev(z, target)
+        )
+
+    def near_in(way):
+        target = right if way == 0 else left
+        return remote(
+            nsub.at[target], grid.at[x, sub_rows(y, core)], i_send.at[2 + way], i_recv.at[2 + way], seq_dev(z, target)
+        )
+
+    def y_copy(xs, yc, h, slot, target):
+        ref = grid.at[xs, sub_rows(yc, core, h)]
+        return remote(ref, ref, y_send.at[xs, h, slot], y_recv.at[xs, yc, h], mp_dev(target, zh, core))
+
+    def e_copy(xs, yc, cc):
+        ref = grid.at[xs, sub_rows(yc, cc)]
+        return remote(ref, ref, e_send.at[xs, yc], e_recv.at[xs, yc], mp_dev(y, zh, 1 - core))
+
+    def normed(block):
+        wide = block.astype(F32)
+        mean = jnp.mean(wide * wide, axis=-1, keepdims=True)
+        return (wide * lax.rsqrt(mean + EPS) * gain_ref[...]).astype(BF16)
+
+    def quarter(ref_slot, rows, value, q):
+        for zs in range(NZ):
+            c = (zs * NX + q) * shard
+            grid_or_sub, slot = ref_slot
+            grid_or_sub[slot, rows, zs * shard:(zs + 1) * shard] = value[:, c:c + shard]
+
+    loads[0].wait()
+    z_start(w_copy, zw_send, 0, (1, 2))
+    loads[1].wait()
+
+    @pl.loop(0, sub // 16)
     def _(i):
         rows = pl.ds(pl.multiple_of(i * 16, 16), 16)
-        wide = xin[rows, :].astype(F32)
-        mean = jnp.mean(wide * wide, axis=-1, keepdims=True)
-        xin[rows, :] = (wide * lax.rsqrt(mean + EPS) * gain_ref[...]).astype(BF16)
-
+        value = normed(xsub[rows, :])
+        for q in range(NX):
+            quarter((nsub, q), rows, value, q)
+
+    far_in(0).start()
+    far_in(1).start()
+    near_in(0).start()
+    near_in(1).start()
+    loads[2].wait()
+    c_copy(0, x, 0).start()
+    c_copy(0, x, 1).start()
+    loads[3].wait()
+    for q in range(NX):
+
+        @pl.when(x == q)
+        def _():
+            @pl.loop(0, tok // 16)
+            def _(i):
+                rows = pl.ds(pl.multiple_of(i * 16, 16), 16)
+                quarter((grid, q), rows, normed(xin[rows, :]), q)
+
+    for way in (0, 1):
+        far_in(way).wait_recv()
+        pass_in(way).start()
+    loads[4].wait()
+    c_copy(1, x, 0).start()
+    c_copy(1, x, 1).start()
+    w_step(1, 1)
+    z_start(w_copy, zw_send, 0, (0,))
+    for way, xs in ((0, left), (1, right)):
+        near_in(way).wait_recv()
+        for h in (0, 1):
+            y_copy(xs, y, h, 0, y_up).start()
+            y_copy(xs, y, h, 1, y_dn).start()
+        e_copy(xs, y, core).start()
     for kind in (0, 1):
         source = left if kind == 0 else right
         c_copy(kind, source, kind).wait_recv()
         c_copy(kind, source, kind).start()
-    x_own(w_copy, w_send, 0)
+    w_step(2, 1)
+    w_step(1, 2)
+    for way in (0, 1):
+        pass_in(way).wait_recv()
+        y_copy(opp, y, way, 0, y_up).start()
+        y_copy(opp, y, way, 1, y_dn).start()
+    e_copy(opp, y, core).start()
+    for xs in (left, right, opp):
+        for h in (0, 1):
+            source, target = (y_dn, y_up) if h == 0 else (y_up, y_dn)
+            y_copy(xs, source, h, 2, target).wait_recv()
+            y_copy(xs, source, h, 2, target).start()
+        for h in (0, 1):
+            y_copy(xs, y_up if h == 0 else y_dn, h, 2, y_up).wait_recv()
+        e_copy(xs, y_dn, core).start()
+        e_copy(xs, y_up, core).start()
     for kind in (0, 1):
         c_copy(kind, right if kind == 0 else left, 0).wait_recv()
     for kind in (0, 1):
@@ -244,52 +327,87 @@
                     for kind in (0, 1):
                         message(buffer, way, d, kind).wait_send()
 
-    def multiply(j):
-        zs = order(j)
-        width = NX * shard
-        span = pl.ds(pl.multiple_of(zs * width, 128), width)
-
+    p_half = tok // 2
+
+    def p_far_copy(k, way):
+        return remote(
+            pout.at[k, opp, pl.ds(way * p_half, p_half)], p_far.at[k, way], r_send.at[k, way], r_recv.at[k, way],
+            seq_dev(z, right if way == 0 else left),
+        )
+
+    def p_close_copy(k, way, h):
+        target = right if way == 0 else left
+        rows = pl.ds(h * p_half, p_half)
+        return remote(
+            pout.at[k, target, rows], p_close.at[k, way, rows], s_send.at[k, way, h], s_recv.at[k, way, h],
+            seq_dev(z, target),
+        )
+
+    def product(k, xs, keep):
         @pl.loop(0, tok // 128)
         def _(i):
             rows = pl.ds(pl.multiple_of(i * 128, 128), 128)
-            for k in range(3):
-                got = jnp.dot(
-                    xin[rows, span], wall[k, pl.ds(pl.multiple_of(zs * width, 16), width), :],
-                    preferred_element_type=F32,
-                )
-                if j == 0:
-                    acc[k, rows, :] = got
-                elif j < NZ - 1:
-                    acc[k, rows, :] += got
-                else:
-                    proj_ref[k, rows, :] = (acc[k, rows, :] + got).astype(BF16)
+            got = jnp.dot(grid[xs, rows, :], wall[k], preferred_element_type=F32)
+            if keep:
+                own[k, rows, :] = got
+            else:
+                pout[k, xs, rows, :] = got.astype(BF16)
+
+    def multiply(k):
+        product(k, opp, False)
+        p_far_copy(k, 0).start()
+        p_far_copy(k, 1).start()
+        product(k, right, False)
+        p_close_copy(k, 0, 1).start()
+        product(k, left, False)
+        p_close_copy(k, 1, 0).start()
+        product(k, x, True)
+
+    def combine(k):
+        for way in (0, 1):
+            target = right if way == 0 else left
+            rows = pl.ds(way * p_half, p_half)
+            p_far_copy(k, way).wait_recv()
+            pout[k, target, rows, :] = (
+                pout[k, target, rows, :].astype(F32) + p_far[k, way].astype(F32)
+            ).astype(BF16)
+            p_close_copy(k, way, way).start()
+
+    def collect(k):
+        for way in (0, 1):
+            for h in (0, 1):
+                p_close_copy(k, way, h).wait_recv()
+        proj_ref[k] = (own[k] + p_close[k, 0].astype(F32) + p_close[k, 1].astype(F32)).astype(BF16)
 
     relay(0, 0)
     relay(1, 0)
-    z_arrive(w_copy, zw_send, 1)
-    z_start(w_copy, zw_send, 1)
-    x_own(w_copy, w_send, 1)
-    x_near(w_copy, w_send, 0)
+    loads[5].wait()
+    z_start(oz_copy, zo_send, 0, (0, 1))
+    x_own(0)
+    w_step(3, 1)
+    w_step(2, 2)
+    w_step(1, 0)
+    for xs in (left, right, opp):
+        for h in (0, 1):
+            y_copy(xs, y_opp, h, 2, y_up).wait_recv()
+        e_copy(xs, y_opp, core).start()
+    for xs in (left, right, opp):
+        for yc in range(4):
+            e_copy(xs, yc, 1 - core).wait_recv()
     relay(0, 1)
     relay(1, 1)
-    z_arrive(w_copy, zw_send, 2)
-    z_start(w_copy, zw_send, 2)
-    x_own(w_copy, w_send, 2)
-    loads[3].wait()
-    z_start(o_copy, zo_send, 0)
-    x_far(w_copy, w_send, 0)
-    multiply(0)
-    x_near(w_copy, w_send, 1)
+    multiply(1)
+    w_step(3, 2)
+    w_step(2, 0)
+    combine(1)
     relay(0, 2)
     relay(1, 2)
-    z_arrive(w_copy, zw_send, 3)
-    z_start(w_copy, zw_send, 3)
-    x_own(w_copy, w_send, 3)
-    x_far(w_copy, w_send, 1)
-    multiply(1)
-    x_near(w_copy, w_send, 2)
+    multiply(2)
+    w_step(3, 0)
+    combine(2)
     relay(0, 3)
     relay(1, 3)
+    multiply(0)
 
     for kind in (0, 1):
         for i in (0, 1):
@@ -307,28 +425,40 @@
     for kind in (0, 1):
         f_copy(kind, x, 0, right).start()
         f_copy(kind, x, 1, left).start()
-    x_own(o_copy, o_send, 0)
+    combine(0)
     for j in (1, 2, 3):
-        z_arrive(o_copy, zo_send, j)
-        z_start(o_copy, zo_send, j)
-        x_own(o_copy, o_send, j)
-    x_far(w_copy, w_send, 2)
-    multiply(2)
-    x_near(w_copy, w_send, 3)
+        z_arrive(oz_copy, zo_send, j, (0, 1))
+        z_start(oz_copy, zo_send, j, (0, 1))
+        x_own(j)
     for kind in (0, 1):
         source, target = (left, right) if kind == 0 else (right, left)
         f_copy(kind, source, 2, target).wait_recv()
         f_copy(kind, source, 2, target).start()
     for j in range(NZ):
-        x_near(o_copy, o_send, j)
-    x_far(w_copy, w_send, 3)
-    multiply(3)
+        x_near(j)
+    for k in (1, 2, 0):
+        collect(k)
     for kind in (0, 1):
         f_copy(kind, right if kind == 0 else left, 2, right).wait_recv()
         f_copy(kind, opp, 2, right).wait_recv()
     for j in range(NZ):
-        x_far(o_copy, o_send, j)
-
+        x_far(j)
+
+    for way in (0, 1):
+        far_in(way).wait_send()
+        pass_in(way).wait_send()
+        near_in(way).wait_send()
+    for xs in (left, right, opp):
+        for h in (0, 1):
+            for slot in range(3):
+                y_copy(xs, y, h, slot, y_up).wait_send()
+        for yc in range(4):
+            e_copy(xs, yc, core).wait_send()
+    for k in range(3):
+        for way in (0, 1):
+            p_far_copy(k, way).wait_send()
+            for h in (0, 1):
+                p_close_copy(k, way, h).wait_send()
     for kind in (0, 1):
         for way in (0, 1):
             c_copy(kind, x, way).wait_send()
@@ -337,10 +467,9 @@
             f_copy(kind, x, slot, right).wait_send()
     relay_finish(0)
     relay_finish(1)
-    z_finish(w_copy, zw_send)
-    x_finish(w_copy, w_send)
-    z_finish(o_copy, zo_send)
-    x_finish(o_copy, o_send)
+    z_finish(w_copy, zw_send, (0, 1, 2))
+    z_finish(oz_copy, zo_send, (0, 1))
+    x_finish()
 
 
 def attend_kernel(
@@ -547,17 +676,26 @@
         out_specs=(vmem(), vmem(), vmem()),
         scratch_shapes=[
             pltpu.VMEM((tok, d_in), BF16),
-            pltpu.VMEM((3, d_in, HD), BF16),
+            pltpu.VMEM((tok // 8, d_in), BF16),
+            pltpu.VMEM((NX, tok // 8, d_in // NX), BF16),
+            pltpu.VMEM((2, tok // 16, d_in // NX), BF16),
+            pltpu.VMEM((NX, tok, d_in // NX), BF16),
+            pltpu.VMEM((3, d_in // NX, HD), BF16),
             pltpu.VMEM((2, NX, 2, blk, HD), BF16),
             pltpu.VMEM((NZ, 2, 2, blk, HD), BF16),
             pltpu.VMEM((NZ, 2, 2, blk, HD), BF16),
             pltpu.VMEM((3, tok, HD), F32),
-            dma((4,)), dma,
+            pltpu.VMEM((3, NX, tok, HD), BF16),
+            pltpu.VMEM((3, 2, tok // 2, HD), BF16),
+            pltpu.VMEM((3, 2, tok, HD), BF16),
+            dma((6,)), dma((4, 3)), dma((4, 3, 2)),
             dma((16, 2)), dma((4, 2, 3)), dma((4, 2, 2)),
-            dma((16, 2)), dma((4, 2, 3)), dma((4, 2, 2)),
+            dma((4,)), dma((4,)), dma((2,)), dma((2,)),
+            dma((4, 4, 2)), dma((4, 2, 3)), dma((4, 4)), dma((4, 4)),
             dma((2, 4)), dma((2, 2, 2)),
             dma((2, 4, 2)), dma((2, 4, 2)),
             dma((2, 4)), dma((2, 3)),
+            dma((3, 2)), dma((3, 2)), dma((3, 2, 2)), dma((3, 2, 2)),
         ],
         compiler_params=pltpu.CompilerParams(
             collective_id=0, has_side_effects=True, vmem_limit_bytes=VMEM_LIMIT

time: 241 us -> 218 us (0.905)
  Pallas kernels: 227 us -> 204 us
    pallas_call x1, Pallas kernels: 164 us -> 145 us  [per_device(): pl.pallas_call(gather_kernel, out_shape=(jax.ShapeDtypeStruct((3, tok, HD...]
    pallas_call x1, Pallas kernels: 62.7 us -> 59 us  [per_device(): pl.pallas_call(attend_kernel, out_shape=jax.ShapeDtypeStruct((tok, HD), B...]
where the time goes in v2:
time: 218 us; the launch traced here: 215 us
  Pallas kernels  204 us (94%)
  local copies, waits for them, and re-layouts  5.44 us (2%)
  other arithmetic  2.85 us (1%)
  matrix products  2.39 us (1%)
    pallas_call x1, Pallas kernels, per_device(): pl.pallas_call(gather_kernel, out_shape=(jax.ShapeDtypeStruct((3, tok, HD...  145 us
    pallas_call x1, Pallas kernels, per_device(): pl.pallas_call(attend_kernel, out_shape=jax.ShapeDtypeStruct((tok, HD), B...  59 us

profile of v2, /device:TPU:2, one launch (start us, length us, event | category | flops | bytes accessed | tf_op | source)
XLA Modules:
  0.0 214.7 jit_solution(7237426641359747886)
XLA Ops:
  0.0 0.0 copy-start
  0.0 1.3 fusion.3
  1.3 0.1 iota_add_fusion
  1.4 0.1 add.52
  1.5 0.8 select_reduce_fusion
  2.4 0.6 pad_add_fusion.table
  2.9 1.8 copy.20.ck_hbm
  4.7 1.8 copy.21.cv_hbm
  6.5 0.0 copy-done
  6.5 2.4 %fusion.1.w_hbm = bf16[3,448,224]{2,1,0:T(8,128)(2,1)} fusion(bf16[3,128,224]{1,2,0:T(8,128)(2,1)S(1)} %copy-done, bf16[448,3,224]{2,0,1:T(8,128)(2,1)} %param.12, bf16[448,128]{1,0:T(8,128)(2,1)} %param.13), kind=kOutput, calls=%fused_computation.2 | convolution fusion | flops 77973504 | bytes 1490944 | tf_op jit(solution)/shard_map/rj,kjc->krc/dot_general | solution.py:656
  8.9 145.1 %gather.1 = (bf16[3,512,224]{2,1,0:T(8,128)(2,1)}, bf16[2,8,256,224]{3,2,1,0:T(8,128)(2,1)}, bf16[16,224,224]{2,1,0:T(8,128)(2,1)}) custom-call(s32[16]{0:T(128)} %pad_add_fusion.table, bf16[512,7168]{1,0:T(8,128)(2,1)} %x_hbm.1, f32[1,7168]{1,0:T(1,128)} %bitcast.16, bf16[3,448,224]{2,1,0:T(8,128)(2,1)} %fusion.1.w_hbm, bf16[2,256,224]{2,1,0:T(8,128)(2,1)} %copy.20.ck_hbm, ...), custom_call_target="tpu_custom_call" | custom-call | tf_op jit(solution)/shard_map/gather/pallas_call | solution.py:668
  154.0 59.0 %attend.1 = bf16[512,224]{1,0:T(8,128)(2,1)} custom-call(s32[1]{0:T(128)} %bitcast.length, bf16[3,512,224]{2,1,0:T(8,128)(2,1)} %get-tuple-element.8.proj_ref, bf16[2,8,256,224]{3,2,1,0:T(8,128)(2,1)} %get-tuple-element.9.kv_ref, bf16[16,224,224]{2,1,0:T(8,128)(2,1)} %get-tuple-element.10.og_ref), custom_call_target="tpu_custom_call" | custom-call | tf_op jit(solution)/shard_map/attend/pallas_call | solution.py:706
  212.9 1.8 copy.22
  (2 shorter events, 0.0 us)
Async XLA Ops:
  0.0 6.5 %copy-start = (bf16[3,128,224]{1,2,0:T(8,128)(2,1)S(1)}, bf16[3,128,224]{1,2,0:T(8,128)(2,1)}, u32[]{:S(2)}) copy-start(bf16[3,128,224]{1,2,0:T(8,128)(2,1)} %param.14) | copy-start | bytes 516100
